TPU v7x, 32 devices: a whole 2x2x4 slice. The times are simulated.
32 devices in a mesh: blk: 8 (over y, x, core), mod: 4 (over z).
Axes of the slice: x: 2, y: 2, z: 4, core: 2. Of those that a mesh axis runs over, the one named last changes fastest.
Arguments:
- act: bfloat16 [4, 32, 8192], P('mod', None, 'blk'), may hold values from -6 to 6
- grad: bfloat16 [4, 64, 8192], P('mod', None, 'blk'), may hold values from -40 to 40
- train: bfloat16 [4, 16384, 2048], P('mod', 'blk'), may hold values from -24 to 24
- pre_out: float32 [4, 64, 64], P('mod'), may hold values from -0.75 to 0.75
- pre_in: float32 [4, 32, 32], P('mod'), may hold values from -1 to 1
- doc_ids: int32 [8192, 1], P('blk'), may hold values from 0 to 255; in each aligned block of 1024 rows (0 to 1023, 1024 to 2047, ...) at most 4 rows name the same one
- owners: int32 [256], replicated, may hold values from 0 to 255, each once
Outputs:
- scores: float32 [4, 256, 16384], P('mod', None, 'blk')
Inputs may be any that keep to these rules, and one draw needn't show every extreme that they name: `doc_ids`: among the 1024 tokens of one index of blk no document has more than 4 tokens, and some document has exactly 4 in some such block; every document has at least one token. `owners`: A permutation of the 256 documents.
All inputs are finite; a program needn't handle non-finite values.
Results may differ from a plain program's by a relative error of at most 0.0029.
Values may be sent and summed in bfloat16 or wider, within the bound.
A program may use at most 64 MiB of HBM per device.

v0:
```python
import functools

import jax
import jax.numpy as jnp
from jax import lax
from jax.experimental import pallas as pl
from jax.experimental.pallas import tpu as pltpu
from jax.sharding import PartitionSpec as P

MOST = 4
LANES = 128
WIDE = 256
CHUNKS = 4
UNROLL = 8
NT = (((1,), (1,)), ((), ()))
TN = (((0,), (0,)), ((), ()))
HIGH = lax.Precision.HIGHEST


def kernel(
    blocks, mods,
    ids_hbm, own_hbm, act_hbm, grad_hbm, pre_out_hbm, pre_in_hbm, train_ref,
    acc, norms,
    ids_ref, own_ref, act_ref, grad_ref, pre_out_ref, pre_in_ref, train_v, send, recv, kin, lay, gath, sq_out, sq_in, tot,
    t_sem, i_sem, sa, ra, sg, rg, sp, rp, sn, rn, st, rt,
):
    a_dim, tokens = act_hbm.shape
    g_dim = grad_hbm.shape[0]
    docs = own_hbm.shape[1]
    per = docs // blocks
    slots = per * MOST
    chips = blocks // 2
    feats = a_dim * g_dim
    part = feats // CHUNKS
    rows_all = train_ref.shape[0]
    tiles = rows_all // WIDE
    packs = LANES // a_dim
    band = WIDE // a_dim
    groups = per // band
    steps = g_dim // packs

    blk = lax.axis_index("blk")
    mod = lax.axis_index("mod")
    chip = lax.div(blk, 2)
    core = lax.rem(blk, 2)
    mate = chip * 2 + (1 - core)

    loads = [
        pltpu.make_async_copy(
            train_ref.at[pl.ds(i * WIDE, WIDE)], train_v.at[pl.ds(i * WIDE, WIDE)], t_sem.at[i]
        )
        for i in range(tiles)
    ]
    barrier = pltpu.get_barrier_semaphore()
    for d in range(1, blocks):
        pl.semaphore_signal(barrier, inc=1, device_id={"blk": lax.rem(blk + d, blocks)}, device_id_type=pl.DeviceIdType.MESH)
    for d in range(1, mods):
        pl.semaphore_signal(barrier, inc=1, device_id={"mod": lax.rem(mod + d, mods)}, device_id_type=pl.DeviceIdType.MESH)
    small = [
        pltpu.make_async_copy(src, dst, i_sem.at[i])
        for i, (src, dst) in enumerate((
            (ids_hbm, ids_ref), (own_hbm, own_ref), (act_hbm, act_ref),
            (grad_hbm, grad_ref), (pre_out_hbm, pre_out_ref), (pre_in_hbm, pre_in_ref)))
    ]
    for load in small + loads:
        load.start()
    small[0].wait()
    small[1].wait()

    ids = ids_ref[...].astype(jnp.float32)
    own_t = jnp.transpose(jnp.broadcast_to(own_ref[...].astype(jnp.float32), (WIDE, docs)))
    before_t = (
        lax.broadcasted_iota(jnp.int32, (WIDE, WIDE), 0) < lax.broadcasted_iota(jnp.int32, (WIDE, WIDE), 1)
    ).astype(jnp.float32).astype(jnp.bfloat16)
    place = lax.broadcasted_iota(jnp.int32, (docs, WIDE), 0).astype(jnp.float32) * MOST
    carry = jnp.zeros((docs, 1), jnp.float32)
    slot_parts = []
    for t in range(tokens // WIDE):
        match = own_t == ids[:, t * WIDE:(t + 1) * WIDE]
        hot = jnp.where(match, 1.0, 0.0)
        before = jnp.dot(hot.astype(jnp.bfloat16), before_t, preferred_element_type=jnp.float32)
        slot_parts.append(jnp.sum(jnp.where(match, place + before + carry, 0.0), axis=0, keepdims=True))
        carry = carry + jnp.sum(hot, axis=1, keepdims=True)
    slot = jnp.concatenate(slot_parts, axis=1).astype(jnp.int32)
    small[2].wait()
    small[3].wait()
    token_rows = jnp.concatenate([act_ref[...], grad_ref[...]], axis=0)

    def a2a(c, k, dest, src):
        return pltpu.make_async_remote_copy(
            src_ref=send.at[c, k], dst_ref=recv.at[src], send_sem=sa.at[c, k],
            recv_sem=ra.at[c, core], device_id={"blk": dest}, device_id_type=pl.DeviceIdType.MESH)

    line = lax.broadcasted_iota(jnp.int32, (2 * slots, tokens), 0)
    sent = []
    for c in list(range(1, chips)) + [0]:
        to = lax.rem(chip + c, chips)
        hot = jnp.where(line == slot - to * (2 * slots), 1.0, 0.0).astype(jnp.bfloat16)
        packed = lax.dot_general(token_rows, hot, NT, preferred_element_type=jnp.float32).astype(jnp.bfloat16)
        halves = [packed[:, :slots], packed[:, slots:]]
        if c:
            for k in range(2):
                send[c, k] = halves[k]
                sent.append(a2a(c, k, to * 2 + k, blk))
        else:
            first = core == 0
            send[0, 0] = jnp.where(first, halves[1], halves[0])
            sent.append(a2a(0, 0, mate, blk))
            recv[blk] = jnp.where(first, halves[0], halves[1])

    pl.semaphore_wait(barrier, blocks + mods - 2)
    for copy in sent:
        copy.start()

    row_w = lax.broadcasted_iota(jnp.int32, (WIDE, WIDE), 0)
    col_w = lax.broadcasted_iota(jnp.int32, (WIDE, WIDE), 1)
    small[4].wait()
    small[5].wait()
    tall = jnp.concatenate([pre_in_ref[...]] * band, axis=0)
    kin[...] = jnp.where(row_w // a_dim == col_w // a_dim, jnp.concatenate([tall] * band, axis=1), 0.0)
    left = jnp.concatenate([pre_out_ref[pl.ds(i, steps, stride=packs), :] for i in range(packs)], axis=0)
    spread = (
        lax.broadcasted_iota(jnp.int32, (a_dim, WIDE), 0) == lax.broadcasted_iota(jnp.int32, (a_dim, WIDE), 1) % a_dim
    ).astype(jnp.float32).astype(jnp.bfloat16)
    span = band * MOST
    slot_doc = (lax.broadcasted_iota(jnp.int32, (slots, WIDE), 0) % span) // MOST
    in_doc = (slot_doc == lax.broadcasted_iota(jnp.int32, (slots, WIDE), 1) // a_dim).astype(jnp.float32)
    slot_group = lax.broadcasted_iota(jnp.int32, (g_dim, slots), 1) // span
    in_group = [(slot_group == q).astype(jnp.float32).astype(jnp.bfloat16) for q in range(groups)]

    def wait_tokens(c, k):
        src = lax.rem(chip - c + chips, chips) * 2 + k
        pltpu.make_async_remote_copy(
            src_ref=send.at[0, 0], dst_ref=recv.at[src], send_sem=sa.at[0, 0],
            recv_sem=ra.at[c, k], device_id={"blk": src}, device_id_type=pl.DeviceIdType.MESH).wait_recv()

    wait_tokens(0, 1 - core)
    for c in range(1, chips):
        for k in range(2):
            wait_tokens(c, k)

    rights, lefts = [], []
    for s in range(blocks):
        wide = lax.dot_general(recv[s, :a_dim, :], spread, TN, preferred_element_type=jnp.float32)
        rights.append((wide * in_doc).astype(jnp.bfloat16))
        y = recv[s, a_dim:, :]
        lefts.append(jnp.concatenate([y * m for m in in_group], axis=0))
    doc_grad = jnp.dot(
        jnp.concatenate(lefts, axis=1), jnp.concatenate(rights, axis=0), preferred_element_type=jnp.float32)
    half = jnp.concatenate(
        [jnp.dot(left, doc_grad[q * g_dim:(q + 1) * g_dim], precision=HIGH, preferred_element_type=jnp.float32)
         for q in range(groups)], axis=0)
    cond = jnp.dot(half, kin[...], precision=HIGH, preferred_element_type=jnp.float32)

    rows = groups * steps
    lane_pack = lax.broadcasted_iota(jnp.int32, (rows, LANES), 1) // a_dim
    for side in range(WIDE // LANES):
        outs = [None] * packs
        for i in range(packs):
            x = jnp.concatenate(
                [cond[q * g_dim + i * steps:q * g_dim + (i + 1) * steps, side * LANES:(side + 1) * LANES]
                 for q in range(groups)], axis=0)
            for pos in range(packs):
                turn = ((i - pos) % packs) * a_dim
                moved = pltpu.roll(x, turn, 1) if turn else x
                outs[pos] = moved if outs[pos] is None else jnp.where(lane_pack == i, moved, outs[pos])
        for pos in range(packs):
            lay[pl.ds((side * packs + pos) * rows, rows), :] = outs[pos]

    def block_rows(b):
        return pl.ds(pl.multiple_of(b * per, per), per)

    def across(ch, c):
        mine = gath.at[ch, block_rows(blk)]
        return pltpu.make_async_remote_copy(
            src_ref=mine, dst_ref=mine, send_sem=sg.at[ch, c], recv_sem=rg.at[ch, c],
            device_id={"blk": lax.rem(chip + c, chips) * 2 + core}, device_id_type=pl.DeviceIdType.MESH)

    def came(ch, c):
        theirs = gath.at[ch, block_rows(lax.rem(chip - c + chips, chips) * 2 + core)]
        return pltpu.make_async_remote_copy(
            src_ref=theirs, dst_ref=theirs, send_sem=sg.at[ch, c], recv_sem=rg.at[ch, c],
            device_id={"blk": lax.rem(chip + c, chips) * 2 + core}, device_id_type=pl.DeviceIdType.MESH)

    def pass_on(ch, c, side):
        it = gath.at[ch, block_rows(lax.rem(chip - c + chips, chips) * 2 + side)]
        return pltpu.make_async_remote_copy(
            src_ref=it, dst_ref=it, send_sem=sp.at[ch, c], recv_sem=rp.at[ch, c],
            device_id={"blk": mate}, device_id_type=pl.DeviceIdType.MESH)

    squares = jnp.zeros((per, LANES), jnp.float32)
    per_chunk = part // LANES
    for ch in range(CHUNKS):
        for u in range(per_chunk):
            j = ch * per_chunk + u
            tile = jnp.concatenate(
                [lay[pl.ds(q * steps + j, band, stride=rows), :] for q in range(groups)], axis=0)
            squares = squares + tile * tile
            gath[ch, block_rows(blk), pl.ds(u * LANES, LANES)] = tile.astype(jnp.bfloat16)
        for c in range(1, chips):
            copy = across(ch, c)
            copy.start()
            sent.append(copy)
        copy = pass_on(ch, 0, core)
        copy.start()
        sent.append(copy)
    sq_out[...] = jnp.broadcast_to(jnp.sum(squares, axis=1, keepdims=True), (per, LANES))

    def square_copy(d):
        return pltpu.make_async_remote_copy(
            src_ref=sq_out, dst_ref=sq_in.at[d], send_sem=sn.at[d], recv_sem=rn.at[d],
            device_id={"mod": lax.rem(mod + d, mods)}, device_id_type=pl.DeviceIdType.MESH)

    def total_copy(d, src):
        return pltpu.make_async_remote_copy(
            src_ref=tot, dst_ref=norms.at[block_rows(src)], send_sem=st.at[d], recv_sem=rt.at[d],
            device_id={"blk": lax.rem(blk + d, blocks)}, device_id_type=pl.DeviceIdType.MESH)

    for d in range(1, mods):
        copy = square_copy(d)
        copy.start()
        sent.append(copy)

    def forward(ch):
        for c in range(1, chips):
            came(ch, c).wait_recv()
            copy = pass_on(ch, c, core)
            copy.start()
            sent.append(copy)

    def multiply(ch):
        for c in range(chips):
            pass_on(ch, c, 1 - core).wait_recv()
        if ch == 0:
            for load in loads:
                load.wait()

        @pl.loop(0, tiles, unroll=UNROLL)
        def _(i):
            at = pl.ds(pl.multiple_of(i * WIDE, WIDE), WIDE)
            product = lax.dot_general(
                gath[ch], train_v[at, ch * part:(ch + 1) * part], NT, preferred_element_type=jnp.float32)
            if ch == 0:
                acc[:, at] = product
            else:
                acc[:, at] = acc[:, at] + product

    forward(0)
    for d in range(1, mods):
        square_copy(d).wait_recv()
    total = sq_out[...]
    for d in range(1, mods):
        total = total + sq_in[d]
    tot[...] = total
    norms[block_rows(blk), :] = total
    for d in range(1, blocks):
        copy = total_copy(d, blk)
        copy.start()
        sent.append(copy)
    for ch in range(CHUNKS):
        if ch + 1 < CHUNKS:
            forward(ch + 1)
        multiply(ch)
    for d in range(1, blocks):
        total_copy(d, lax.rem(blk - d + blocks, blocks)).wait_recv()
    for copy in sent:
        copy.wait_send()


def body(blocks, mods, act, grad, train, pre_out, pre_in, doc_ids, owners):
    a_dim, tokens = act.shape[1:]
    g_dim = grad.shape[1]
    docs = owners.shape[0]
    per = docs // blocks
    chips = blocks // 2
    feats = a_dim * g_dim
    part = feats // CHUNKS
    rows = train.shape[1]
    tiles = rows // WIDE
    slots = per * MOST
    band = WIDE // a_dim
    vmem = pl.BlockSpec(memory_space=pltpu.VMEM)
    hbm = pl.BlockSpec(memory_space=pltpu.HBM)
    dma = pltpu.SemaphoreType.DMA
    raw, norms = pl.pallas_call(
        functools.partial(kernel, blocks, mods),
        out_shape=(
            jax.ShapeDtypeStruct((docs, rows), jnp.float32),
            jax.ShapeDtypeStruct((docs, LANES), jnp.float32),
        ),
        in_specs=[hbm] * 7,
        out_specs=(vmem, vmem),
        scratch_shapes=[
            pltpu.VMEM((1, tokens), jnp.int32),
            pltpu.VMEM((1, docs), jnp.int32),
            pltpu.VMEM((a_dim, tokens), jnp.bfloat16),
            pltpu.VMEM((g_dim, tokens), jnp.bfloat16),
            pltpu.VMEM((g_dim, g_dim), jnp.float32),
            pltpu.VMEM((a_dim, a_dim), jnp.float32),
            pltpu.VMEM((rows, feats), jnp.bfloat16),
            pltpu.VMEM((chips, 2, a_dim + g_dim, slots), jnp.bfloat16),
            pltpu.VMEM((blocks, a_dim + g_dim, slots), jnp.bfloat16),
            pltpu.VMEM((WIDE, WIDE), jnp.float32),
            pltpu.VMEM((per * g_dim * a_dim // LANES, LANES), jnp.float32),
            pltpu.VMEM((CHUNKS, docs, part), jnp.bfloat16),
            pltpu.VMEM((per, LANES), jnp.float32),
            pltpu.VMEM((mods, per, LANES), jnp.float32),
            pltpu.VMEM((per, LANES), jnp.float32),
            dma((tiles,)), dma((6,)),
            dma((chips, 2)), dma((chips, 2)),
            dma((CHUNKS, chips)), dma((CHUNKS, chips)),
            dma((CHUNKS, chips)), dma((CHUNKS, chips)),
            dma((mods,)), dma((mods,)),
            dma((blocks,)), dma((blocks,)),
        ],
        compiler_params=pltpu.CompilerParams(
            collective_id=0, has_side_effects=True, vmem_limit_bytes=48 * 1024 * 1024),
    )(*[pltpu.with_memory_space_constraint(x, pltpu.HBM) for x in (
        doc_ids.reshape(1, tokens), owners.reshape(1, docs), act[0], grad[0], pre_out[0], pre_in[0], train[0])])
    return (raw * (1.0 / jnp.sqrt(norms[:, :1] + 1e-06)))[None]


def solution(mesh):
    blocks, mods = mesh.shape["blk"], mesh.shape["mod"]
    return jax.shard_map(
        functools.partial(body, blocks, mods),
        mesh=mesh,
        in_specs=(
            P("mod", None, "blk"),
            P("mod", None, "blk"),
            P("mod", "blk", None),
            P("mod", None, None),
            P("mod", None, None),
            P("blk", None),
            P(),
        ),
        out_specs=P("mod", None, "blk"),
        check_vma=False,
    )
```

profile of v0, /device:TPU:0, one launch (start us, length us, event | category | flops | bytes accessed | tf_op | source)
XLA Modules:
  0.0 23.8 jit_solution(9887123532416974874)
XLA Ops:
  0.0 22.2 %shard_map.73 = (f32[256,2048]{1,0:T(8,128)S(1)}, f32[256,128]{1,0:T(8,128)S(1)}) custom-call(s32[1,1024]{1,0:T(1,128)} %bitcast.14, s32[1,256]{1,0:T(1,128)} %bitcast.15, bf16[32,1024]{1,0:T(8,128)(2,1)} %bitcast.11, bf16[64,1024]{1,0:T(8,128)(2,1)} %bitcast.10, f32[64,64]{1,0:T(8,128)} %bitcast.12, f32[32,32]{1,0:T(8,128)} %bitcast.13, ...), custom_call_target="tpu_custom_call" | custom-call | tf_op jit(solution)/shard_map/pallas_call | solution.py:285
  22.2 0.1 rsqrt_reduce_fusion
  22.3 1.5 %multiply_bitcast_fusion = f32[1,256,2048]{2,1,0:T(8,128)} fusion(f32[256,2048]{1,0:T(8,128)S(1)} %get-tuple-element.7, f32[256]{0:T(256)S(1)} %rsqrt_reduce_fusion), kind=kLoop, calls=%fused_computation | loop fusion | flops 524288 | bytes 4195328 | tf_op jit(solution)/shard_map/broadcast_in_dim | solution.py:320
where the time goes:
time: 24 us; the launch traced here: 23.8 us
  Pallas kernels  22.2 us (92%)
  other arithmetic  1.65 us (7%)
    pallas_call x1, Pallas kernels, body(): pl.pallas_call(functools.partial(kernel, blocks, mods), out_shape=(jax.Sh...  22.2 us
    broadcast_in_dim x1, other arithmetic, body(): return (raw * (1.0 / jnp.sqrt(norms[:, :1] + 1e-06)))[None]  1.53 us

commit v1 on v0

--- a/solution.py
+++ b/solution.py
@@ -22,7 +22,7 @@
     ids_hbm, own_hbm, act_hbm, grad_hbm, pre_out_hbm, pre_in_hbm, train_ref,
     acc, norms,
     ids_ref, own_ref, act_ref, grad_ref, pre_out_ref, pre_in_ref, train_v, send, recv, kin, lay, gath, sq_out, sq_in, tot,
-    t_sem, i_sem, sa, ra, sg, rg, sp, rp, sn, rn, st, rt,
+    t_sem, i_sem, go, sa, ra, sg, rg, sp, rp, sn, rn, st, rt,
 ):
     a_dim, tokens = act_hbm.shape
     g_dim = grad_hbm.shape[0]
@@ -51,19 +51,19 @@
         )
         for i in range(tiles)
     ]
-    barrier = pltpu.get_barrier_semaphore()
-    for d in range(1, blocks):
-        pl.semaphore_signal(barrier, inc=1, device_id={"blk": lax.rem(blk + d, blocks)}, device_id_type=pl.DeviceIdType.MESH)
-    for d in range(1, mods):
-        pl.semaphore_signal(barrier, inc=1, device_id={"mod": lax.rem(mod + d, mods)}, device_id_type=pl.DeviceIdType.MESH)
     small = [
         pltpu.make_async_copy(src, dst, i_sem.at[i])
         for i, (src, dst) in enumerate((
             (ids_hbm, ids_ref), (own_hbm, own_ref), (act_hbm, act_ref),
             (grad_hbm, grad_ref), (pre_out_hbm, pre_out_ref), (pre_in_hbm, pre_in_ref)))
     ]
-    for load in small + loads:
+    for load in small:
         load.start()
+    barrier = pltpu.get_barrier_semaphore()
+    for c in range(chips):
+        @pl.when(c * 2 != blk)
+        def _():
+            pl.semaphore_signal(barrier, inc=1, device_id={"blk": c * 2}, device_id_type=pl.DeviceIdType.MESH)
     small[0].wait()
     small[1].wait()
 
@@ -108,9 +108,26 @@
             sent.append(a2a(0, 0, mate, blk))
             recv[blk] = jnp.where(first, halves[0], halves[1])
 
-    pl.semaphore_wait(barrier, blocks + mods - 2)
+
+    @pl.when(core == 0)
+    def _():
+        pl.semaphore_wait(barrier, blocks - 1)
+        pl.semaphore_signal(go, inc=1, device_id={"blk": mate}, device_id_type=pl.DeviceIdType.MESH)
+
+    @pl.when(core == 1)
+    def _():
+        pl.semaphore_wait(go, 1)
+
     for copy in sent:
         copy.start()
+    for load in loads:
+        load.start()
+
+    @pl.when(core == 1)
+    def _():
+        for d in range(1, mods):
+            pl.semaphore_signal(barrier, inc=1, device_id={"mod": lax.rem(mod + d, mods)}, device_id_type=pl.DeviceIdType.MESH)
+
 
     row_w = lax.broadcasted_iota(jnp.int32, (WIDE, WIDE), 0)
     col_w = lax.broadcasted_iota(jnp.int32, (WIDE, WIDE), 1)
@@ -216,6 +233,15 @@
             src_ref=tot, dst_ref=norms.at[block_rows(src)], send_sem=st.at[d], recv_sem=rt.at[d],
             device_id={"blk": lax.rem(blk + d, blocks)}, device_id_type=pl.DeviceIdType.MESH)
 
+    @pl.when(core == 1)
+    def _():
+        pl.semaphore_wait(barrier, mods - 1)
+        pl.semaphore_signal(go, inc=1, device_id={"blk": mate}, device_id_type=pl.DeviceIdType.MESH)
+
+    @pl.when(core == 0)
+    def _():
+        pl.semaphore_wait(go, 1)
+
     for d in range(1, mods):
         copy = square_copy(d)
         copy.start()
@@ -246,20 +272,21 @@
                 acc[:, at] = acc[:, at] + product
 
     forward(0)
-    for d in range(1, mods):
-        square_copy(d).wait_recv()
-    total = sq_out[...]
-    for d in range(1, mods):
-        total = total + sq_in[d]
-    tot[...] = total
-    norms[block_rows(blk), :] = total
-    for d in range(1, blocks):
-        copy = total_copy(d, blk)
-        copy.start()
-        sent.append(copy)
     for ch in range(CHUNKS):
         if ch + 1 < CHUNKS:
             forward(ch + 1)
+        if ch == 2:
+            for d in range(1, mods):
+                square_copy(d).wait_recv()
+            total = sq_out[...]
+            for d in range(1, mods):
+                total = total + sq_in[d]
+            tot[...] = total
+            norms[block_rows(blk), :] = total
+            for d in range(1, blocks):
+                copy = total_copy(d, blk)
+                copy.start()
+                sent.append(copy)
         multiply(ch)
     for d in range(1, blocks):
         total_copy(d, lax.rem(blk - d + blocks, blocks)).wait_recv()
@@ -285,8 +312,8 @@
     raw, norms = pl.pallas_call(
         functools.partial(kernel, blocks, mods),
         out_shape=(
-            jax.ShapeDtypeStruct((docs, rows), jnp.float32),
-            jax.ShapeDtypeStruct((docs, LANES), jnp.float32),
+            pltpu.VMEM((docs, rows), jnp.float32),
+            pltpu.VMEM((docs, LANES), jnp.float32),
         ),
         in_specs=[hbm] * 7,
         out_specs=(vmem, vmem),
@@ -306,7 +333,7 @@
             pltpu.VMEM((per, LANES), jnp.float32),
             pltpu.VMEM((mods, per, LANES), jnp.float32),
             pltpu.VMEM((per, LANES), jnp.float32),
-            dma((tiles,)), dma((6,)),
+            dma((tiles,)), dma((6,)), pltpu.SemaphoreType.REGULAR,
             dma((chips, 2)), dma((chips, 2)),
             dma((CHUNKS, chips)), dma((CHUNKS, chips)),
             dma((CHUNKS, chips)), dma((CHUNKS, chips)),

time: 24 us -> 24.6 us (1.025)
  Pallas kernels: 22.2 us -> 22.8 us
    pallas_call x1, Pallas kernels: 22.2 us -> 22.8 us  [body(): pl.pallas_call(functools.partial(kernel, blocks, mods), out_shape=(pltpu....]
where the time goes in v1:
time: 24.6 us; the launch traced here: 24.5 us
  Pallas kernels  22.8 us (93%)
  other arithmetic  1.65 us (7%)
    pallas_call x1, Pallas kernels, body(): pl.pallas_call(functools.partial(kernel, blocks, mods), out_shape=(pltpu....  22.8 us
    broadcast_in_dim x1, other arithmetic, body(): return (raw * (1.0 / jnp.sqrt(norms[:, :1] + 1e-06)))[None]  1.53 us

profile of v1, /device:TPU:0, one launch (start us, length us, event | category | flops | bytes accessed | tf_op | source)
XLA Modules:
  0.0 24.5 jit_solution(10554957111982356607)
XLA Ops:
  0.0 22.8 %shard_map.73 = (f32[256,2048]{1,0:T(8,128)S(1)}, f32[256,128]{1,0:T(8,128)S(1)}) custom-call(s32[1,1024]{1,0:T(1,128)} %bitcast.14, s32[1,256]{1,0:T(1,128)} %bitcast.15, bf16[32,1024]{1,0:T(8,128)(2,1)} %bitcast.11, bf16[64,1024]{1,0:T(8,128)(2,1)} %bitcast.10, f32[64,64]{1,0:T(8,128)} %bitcast.12, f32[32,32]{1,0:T(8,128)} %bitcast.13, ...), custom_call_target="tpu_custom_call" | custom-call | tf_op jit(solution)/shard_map/pallas_call | solution.py:312
  22.8 0.1 rsqrt_reduce_fusion
  22.9 1.5 %multiply_bitcast_fusion = f32[1,256,2048]{2,1,0:T(8,128)} fusion(f32[256,2048]{1,0:T(8,128)S(1)} %get-tuple-element.7, f32[256]{0:T(256)S(1)} %rsqrt_reduce_fusion), kind=kLoop, calls=%fused_computation | loop fusion | flops 524288 | bytes 4195328 | tf_op jit(solution)/shard_map/broadcast_in_dim | solution.py:347

commit v2 on v1

v2 whole, which is shorter than its diff:
```python
import functools

import jax
import jax.numpy as jnp
from jax import lax
from jax.experimental import pallas as pl
from jax.experimental.pallas import tpu as pltpu
from jax.sharding import PartitionSpec as P

MOST = 4
LANES = 128
WIDE = 256
CHUNKS = 4
UNROLL = 8
NT = (((1,), (1,)), ((), ()))
TN = (((0,), (0,)), ((), ()))
HIGH = lax.Precision.HIGHEST


def kernel(
    blocks, mods,
    ids_hbm, own_hbm, act_hbm, grad_hbm, pre_out_hbm, pre_in_hbm, train_ref,
    acc, norms, inv, kout, ids_ref, own_ref, act_ref, grad_ref, pre_out_ref, pre_in_ref, train_v, send, recv, kin, lay, gath, sq_out, sq_in, tot,
    t_sem, i_sem, go, sa, ra, sg, rg, rp, sn, rn, st, rt,
):
    a_dim, tokens = act_hbm.shape
    g_dim = grad_hbm.shape[0]
    docs = own_hbm.shape[1]
    per = docs // blocks
    slots = per * MOST
    chips = blocks // 2
    feats = a_dim * g_dim
    part = feats // CHUNKS
    rows_all = train_ref.shape[0]
    tiles = rows_all // WIDE
    packs = LANES // a_dim
    band = WIDE // a_dim
    groups = per // band
    steps = g_dim // packs

    blk = lax.axis_index("blk")
    mod = lax.axis_index("mod")
    chip = lax.div(blk, 2)
    core = lax.rem(blk, 2)
    mate = chip * 2 + (1 - core)
    square = chips == 4
    if square:
        hops = [chip, chip + 1 - 2 * lax.rem(chip, 2), lax.rem(chip + 2, chips), chips - 1 - chip]

    def onto(c):
        return hops[c] if square else lax.rem(chip + c, chips)

    def source(c):
        return hops[c] if square else lax.rem(chip - c + chips, chips)

    order = list(range(chips - 1, 0, -1))

    loads = [
        pltpu.make_async_copy(
            train_ref.at[pl.ds(i * WIDE, WIDE)], train_v.at[pl.ds(i * WIDE, WIDE)], t_sem
        )
        for i in range(tiles)
    ]
    small = [
        pltpu.make_async_copy(src, dst, i_sem.at[i])
        for i, (src, dst) in enumerate((
            (ids_hbm, ids_ref), (own_hbm, own_ref), (act_hbm, act_ref),
            (grad_hbm, grad_ref), (pre_out_hbm, pre_out_ref), (pre_in_hbm, pre_in_ref)))
    ]
    for load in small:
        load.start()
    barrier = pltpu.get_barrier_semaphore()
    for c in range(chips):
        @pl.when(c * 2 != blk)
        def _():
            pl.semaphore_signal(barrier, inc=1, device_id={"blk": c * 2}, device_id_type=pl.DeviceIdType.MESH)
    small[0].wait()
    small[1].wait()

    ids = ids_ref[...].astype(jnp.float32)
    own_t = jnp.transpose(jnp.broadcast_to(own_ref[...].astype(jnp.float32), (WIDE, docs)))
    before_t = (
        lax.broadcasted_iota(jnp.int32, (WIDE, WIDE), 0) < lax.broadcasted_iota(jnp.int32, (WIDE, WIDE), 1)
    ).astype(jnp.float32).astype(jnp.bfloat16)
    place = lax.broadcasted_iota(jnp.int32, (docs, WIDE), 0).astype(jnp.float32) * MOST
    carry = jnp.zeros((docs, 1), jnp.float32)
    slot_parts = []
    for t in range(tokens // WIDE):
        match = own_t == ids[:, t * WIDE:(t + 1) * WIDE]
        hot = jnp.where(match, 1.0, 0.0)
        before = jnp.dot(hot.astype(jnp.bfloat16), before_t, preferred_element_type=jnp.float32)
        slot_parts.append(jnp.sum(jnp.where(match, place + before + carry, 0.0), axis=0, keepdims=True))
        carry = carry + jnp.sum(hot, axis=1, keepdims=True)
    slot = jnp.concatenate(slot_parts, axis=1).astype(jnp.int32)
    small[2].wait()
    small[3].wait()
    token_rows = jnp.concatenate([act_ref[...], grad_ref[...]], axis=0)

    def a2a(c, k, dest, src):
        return pltpu.make_async_remote_copy(
            src_ref=send.at[2 * c + k], dst_ref=recv.at[src], send_sem=sa,
            recv_sem=ra.at[c], device_id={"blk": dest}, device_id_type=pl.DeviceIdType.MESH)

    line = lax.broadcasted_iota(jnp.int32, (2 * slots, tokens), 0)
    for c in order + [0]:
        to = onto(c)
        hot = jnp.where(line == slot - to * (2 * slots), 1.0, 0.0).astype(jnp.bfloat16)
        packed = lax.dot_general(token_rows, hot, NT, preferred_element_type=jnp.float32).astype(jnp.bfloat16)
        halves = [packed[:, :slots], packed[:, slots:]]
        if c == order[0]:

            @pl.when(core == 0)
            def _():
                pl.semaphore_wait(barrier, blocks - 1)
                pl.semaphore_signal(go, inc=1, device_id={"blk": mate}, device_id_type=pl.DeviceIdType.MESH)

            @pl.when(core == 1)
            def _():
                pl.semaphore_wait(go, 1)

        if c:
            for k in range(2):
                send[2 * c + k] = halves[k]
                a2a(c, k, to * 2 + k, blk).start()
        else:
            first = core == 0
            send[0] = jnp.where(first, halves[1], halves[0])
            a2a(0, 0, mate, blk).start()
            recv[blk] = jnp.where(first, halves[0], halves[1])
    for load in loads:
        load.start()

    @pl.when(core == 1)
    def _():
        for d in range(1, mods):
            pl.semaphore_signal(barrier, inc=1, device_id={"mod": lax.rem(mod + d, mods)}, device_id_type=pl.DeviceIdType.MESH)


    row_w = lax.broadcasted_iota(jnp.int32, (WIDE, WIDE), 0)
    col_w = lax.broadcasted_iota(jnp.int32, (WIDE, WIDE), 1)
    small[4].wait()
    small[5].wait()
    tall = jnp.concatenate([pre_in_ref[...]] * band, axis=0)
    right = jnp.where(row_w // a_dim == col_w // a_dim, jnp.concatenate([tall] * band, axis=1), 0.0)
    high = right.astype(jnp.bfloat16)
    low = (right - high.astype(jnp.float32)).astype(jnp.bfloat16)
    kin[...] = jnp.concatenate([high, high, low], axis=0)
    left = jnp.concatenate([pre_out_ref[pl.ds(i, steps, stride=packs), :] for i in range(packs)], axis=0)
    wide_left = jnp.concatenate([left] * groups, axis=0)
    row_q = lax.broadcasted_iota(jnp.int32, (groups * g_dim, groups * g_dim), 0)
    col_q = lax.broadcasted_iota(jnp.int32, (groups * g_dim, groups * g_dim), 1)
    wide_left = jnp.where(row_q // g_dim == col_q // g_dim, jnp.concatenate([wide_left] * groups, axis=1), 0.0)
    high = wide_left.astype(jnp.bfloat16)
    low = (wide_left - high.astype(jnp.float32)).astype(jnp.bfloat16)
    kout[...] = jnp.concatenate([high, high, low], axis=1)
    spread = (
        lax.broadcasted_iota(jnp.int32, (a_dim, WIDE), 0) == lax.broadcasted_iota(jnp.int32, (a_dim, WIDE), 1) % a_dim
    ).astype(jnp.float32).astype(jnp.bfloat16)
    span = band * MOST
    slot_doc = (lax.broadcasted_iota(jnp.int32, (slots, WIDE), 0) % span) // MOST
    in_doc = (slot_doc == lax.broadcasted_iota(jnp.int32, (slots, WIDE), 1) // a_dim).astype(jnp.float32)
    slot_group = lax.broadcasted_iota(jnp.int32, (g_dim, slots), 1) // span
    in_group = [(slot_group == q).astype(jnp.float32).astype(jnp.bfloat16) for q in range(groups)]

    def wait_tokens(c):
        got = recv.at[pl.ds(source(c) * 2, 2)] if c else recv.at[mate]
        pltpu.make_async_copy(got, got, ra.at[c]).wait()

    doc_grad = None
    for c in [0] + order:
        wait_tokens(c)
        rights, lefts = [], []
        for k in range(2):
            s = source(c) * 2 + k
            wide = lax.dot_general(recv[s, :a_dim, :], spread, TN, preferred_element_type=jnp.float32)
            rights.append((wide * in_doc).astype(jnp.bfloat16))
            y = recv[s, a_dim:, :]
            lefts.append(jnp.concatenate([y * m for m in in_group], axis=0))
        part_grad = jnp.dot(
            jnp.concatenate(lefts, axis=1), jnp.concatenate(rights, axis=0), preferred_element_type=jnp.float32)
        doc_grad = part_grad if doc_grad is None else doc_grad + part_grad
    high = doc_grad.astype(jnp.bfloat16)
    low = (doc_grad - high.astype(jnp.float32)).astype(jnp.bfloat16)
    half = jnp.dot(jnp.concatenate([high, low, high], axis=1), kin[...], preferred_element_type=jnp.float32)
    high = half.astype(jnp.bfloat16)
    low = (half - high.astype(jnp.float32)).astype(jnp.bfloat16)
    cond = jnp.dot(kout[...], jnp.concatenate([high, low, high], axis=0), preferred_element_type=jnp.float32)

    rows = groups * steps
    lane_pack = lax.broadcasted_iota(jnp.int32, (rows, LANES), 1) // a_dim
    for side in range(WIDE // LANES):
        outs = [None] * packs
        for i in range(packs):
            x = jnp.concatenate(
                [cond[q * g_dim + i * steps:q * g_dim + (i + 1) * steps, side * LANES:(side + 1) * LANES]
                 for q in range(groups)], axis=0)
            for pos in range(packs):
                turn = ((i - pos) % packs) * a_dim
                moved = pltpu.roll(x, turn, 1) if turn else x
                outs[pos] = moved if outs[pos] is None else jnp.where(lane_pack == i, moved, outs[pos])
        for pos in range(packs):
            lay[pl.ds((side * packs + pos) * rows, rows), :] = outs[pos]

    def block_rows(b):
        return pl.ds(pl.multiple_of(b * per, per), per)

    def block(ch, b):
        return gath.at[ch, block_rows(b)]

    def move(ref, to, got):
        pltpu.make_async_remote_copy(
            src_ref=ref, dst_ref=ref, send_sem=sg, recv_sem=got, device_id={"blk": to},
            device_id_type=pl.DeviceIdType.MESH).start()

    def wait_for(ref, sem):
        pltpu.make_async_copy(ref, ref, sem).wait()

    squares = jnp.zeros((per, LANES), jnp.float32)
    per_chunk = part // LANES
    for ch in range(CHUNKS):
        for u in range(per_chunk):
            j = ch * per_chunk + u
            tile = jnp.concatenate(
                [lay[pl.ds(q * steps + j, band, stride=rows), :] for q in range(groups)], axis=0)
            squares = squares + tile * tile
            gath[ch, block_rows(blk), pl.ds(u * LANES, LANES)] = tile.astype(jnp.bfloat16)
        for c in order:
            move(block(ch, blk), onto(c) * 2 + core, rg.at[ch, c])
        move(block(ch, blk), mate, rp.at[ch])
    sq_out[...] = jnp.broadcast_to(jnp.sum(squares, axis=1, keepdims=True), (per, LANES))

    def square_copy(d):
        return pltpu.make_async_remote_copy(
            src_ref=sq_out, dst_ref=sq_in.at[d], send_sem=sn, recv_sem=rn,
            device_id={"mod": lax.rem(mod + d, mods)}, device_id_type=pl.DeviceIdType.MESH)

    def total_copy(d, src):
        return pltpu.make_async_remote_copy(
            src_ref=tot, dst_ref=norms.at[block_rows(src)], send_sem=st, recv_sem=rt,
            device_id={"blk": lax.rem(blk + d, blocks)}, device_id_type=pl.DeviceIdType.MESH)

    @pl.when(core == 1)
    def _():
        pl.semaphore_wait(barrier, mods - 1)
        pl.semaphore_signal(go, inc=1, device_id={"blk": mate}, device_id_type=pl.DeviceIdType.MESH)

    @pl.when(core == 0)
    def _():
        pl.semaphore_wait(go, 1)

    for d in range(1, mods):
        square_copy(d).start()

    def forward(ch, c):
        b = source(c) * 2 + core
        wait_for(block(ch, b), rg.at[ch, c])
        move(block(ch, b), mate, rp.at[ch])

    def multiply(ch):
        half_of = gath.at[ch, pl.ds(0, docs // 2)]
        wait_for(half_of, rp.at[ch])
        if ch == 0:
            pltpu.make_async_copy(train_ref, train_v, t_sem).wait()

        @pl.loop(0, tiles, unroll=UNROLL)
        def _(i):
            at = pl.ds(pl.multiple_of(i * WIDE, WIDE), WIDE)
            product = lax.dot_general(
                gath[ch], train_v[at, ch * part:(ch + 1) * part], NT, preferred_element_type=jnp.float32)
            if ch == 0:
                acc[:, at] = product
            elif ch < CHUNKS - 1:
                acc[:, at] = acc[:, at] + product
            else:
                acc[:, at] = (acc[:, at] + product) * inv[...]

    def totals():
        wait_for(sq_in.at[pl.ds(1, mods - 1)], rn)
        total = sq_out[...]
        for d in range(1, mods):
            total = total + sq_in[d]
        tot[...] = total
        norms[block_rows(blk), :] = total
        for d in range(1, blocks):
            total_copy(d, blk).start()

    for ch in range(CHUNKS):
        for at in range(ch + (ch > 0), min(ch + 2, CHUNKS)):
            for c in order:
                forward(at, c)
        if ch == 0:
            totals()
        if ch == CHUNKS - 1:
            others = norms.at[pl.ds(0, docs - per)]
            wait_for(others, rt)
            scale = 1.0 / jnp.sqrt(norms[...] + 1e-06)
            inv[...] = jnp.concatenate([scale] * (WIDE // LANES), axis=1)
        multiply(ch)
    wait_for(send.at[pl.ds(0, blocks - 1)], sa)
    wait_for(gath.at[:, pl.ds(0, docs - per)], sg)
    wait_for(sq_in.at[pl.ds(1, mods - 1)], sn)
    wait_for(others, st)


def body(blocks, mods, act, grad, train, pre_out, pre_in, doc_ids, owners):
    a_dim, tokens = act.shape[1:]
    g_dim = grad.shape[1]
    docs = owners.shape[0]
    per = docs // blocks
    chips = blocks // 2
    feats = a_dim * g_dim
    part = feats // CHUNKS
    rows = train.shape[1]
    tiles = rows // WIDE
    slots = per * MOST
    band = WIDE // a_dim
    square_of = per // band * g_dim
    hbm = pl.BlockSpec(memory_space=pltpu.HBM)
    dma = pltpu.SemaphoreType.DMA
    scores = pl.pallas_call(
        functools.partial(kernel, blocks, mods),
        out_shape=pltpu.VMEM((docs, rows), jnp.float32),
        in_specs=[hbm] * 7,
        out_specs=pl.BlockSpec(memory_space=pltpu.VMEM),
        scratch_shapes=[
            pltpu.VMEM((docs, LANES), jnp.float32),
            pltpu.VMEM((docs, WIDE), jnp.float32),
            pltpu.VMEM((square_of, 3 * square_of), jnp.bfloat16),
            pltpu.VMEM((1, tokens), jnp.int32),
            pltpu.VMEM((1, docs), jnp.int32),
            pltpu.VMEM((a_dim, tokens), jnp.bfloat16),
            pltpu.VMEM((g_dim, tokens), jnp.bfloat16),
            pltpu.VMEM((g_dim, g_dim), jnp.float32),
            pltpu.VMEM((a_dim, a_dim), jnp.float32),
            pltpu.VMEM((rows, feats), jnp.bfloat16),
            pltpu.VMEM((blocks, a_dim + g_dim, slots), jnp.bfloat16),
            pltpu.VMEM((blocks, a_dim + g_dim, slots), jnp.bfloat16),
            pltpu.VMEM((3 * WIDE, WIDE), jnp.bfloat16),
            pltpu.VMEM((per * g_dim * a_dim // LANES, LANES), jnp.float32),
            pltpu.VMEM((CHUNKS, docs, part), jnp.bfloat16),
            pltpu.VMEM((per, LANES), jnp.float32),
            pltpu.VMEM((mods, per, LANES), jnp.float32),
            pltpu.VMEM((per, LANES), jnp.float32),
            dma(()), dma((6,)), pltpu.SemaphoreType.REGULAR,
            dma(()), dma((chips,)),
            dma(()), dma((CHUNKS, chips)), dma((CHUNKS,)),
            dma(()), dma(()), dma(()), dma(()),
        ],
        compiler_params=pltpu.CompilerParams(
            collective_id=0, has_side_effects=True, vmem_limit_bytes=48 * 1024 * 1024),
    )(*[pltpu.with_memory_space_constraint(x, pltpu.HBM) for x in (
        doc_ids.reshape(1, tokens), owners.reshape(1, docs), act[0], grad[0], pre_out[0], pre_in[0], train[0])])
    return scores[None]


def solution(mesh):
    blocks, mods = mesh.shape["blk"], mesh.shape["mod"]
    return jax.shard_map(
        functools.partial(body, blocks, mods),
        mesh=mesh,
        in_specs=(
            P("mod", None, "blk"),
            P("mod", None, "blk"),
            P("mod", "blk", None),
            P("mod", None, None),
            P("mod", None, None),
            P("blk", None),
            P(),
        ),
        out_specs=P("mod", None, "blk"),
        check_vma=False,
    )
```

time: 24.6 us -> 21.7 us (0.88)
  Pallas kernels: 22.8 us -> 20.1 us
  other arithmetic: 1.65 us -> 0 us
  local copies, waits for them, and re-layouts: 0 us -> 1.32 us
    pallas_call x1, Pallas kernels: 22.8 us -> 20.1 us  [body(): pl.pallas_call(functools.partial(kernel, blocks, mods), out_shape=pltpu.V...]
    broadcast_in_dim x1 -> x0, other arithmetic: 1.53 us -> none  [body(): return (raw * (1.0 / jnp.sqrt(norms[:, :1] + 1e-06)))[None]]
    unnamed x0 -> x1, local copies, waits for them, and re-layouts: none -> 1.32 us
where the time goes in v2:
time: 21.7 us; the launch traced here: 21.4 us
  Pallas kernels  20.1 us (93%)
  local copies, waits for them, and re-layouts  1.32 us (6%)
    pallas_call x1, Pallas kernels, body(): pl.pallas_call(functools.partial(kernel, blocks, mods), out_shape=pltpu.V...  20.1 us
    unnamed x1, local copies, waits for them, and re-layouts  1.32 us

profile of v2, /device:TPU:0, one launch (start us, length us, event | category | flops | bytes accessed | tf_op | source)
XLA Modules:
  0.0 21.4 jit_solution(18372816589809047187)
XLA Ops:
  0.0 20.1 %shard_map.73 = f32[256,2048]{1,0:T(8,128)S(1)} custom-call(s32[1,1024]{1,0:T(1,128)} %bitcast.14, s32[1,256]{1,0:T(1,128)} %bitcast.15, bf16[32,1024]{1,0:T(8,128)(2,1)} %bitcast.11, bf16[64,1024]{1,0:T(8,128)(2,1)} %bitcast.10, f32[64,64]{1,0:T(8,128)} %bitcast.12, f32[32,32]{1,0:T(8,128)} %bitcast.13, bf16[2048,2048]{1,0:T(8,128)(2,1)} %bitcast.9), custom_call_target="tpu_custom_call" | custom-call | tf_op jit(solution)/shard_map/pallas_call | solution.py:320
  20.1 1.3 %copy.9 = f32[1,256,2048]{2,1,0:T(8,128)} copy(f32[1,256,2048]{2,1,0:T(8,128)S(1)} %bitcast.8) | data formatting | bytes 4194304

commit v3 on v2

--- a/solution.py
+++ b/solution.py
@@ -9,6 +9,7 @@
 
 MOST = 4
 LANES = 128
+SUBLANES = 8
 WIDE = 256
 CHUNKS = 4
 UNROLL = 8
@@ -101,10 +102,12 @@
             src_ref=send.at[2 * c + k], dst_ref=recv.at[src], send_sem=sa,
             recv_sem=ra.at[c], device_id={"blk": dest}, device_id_type=pl.DeviceIdType.MESH)
 
-    line = lax.broadcasted_iota(jnp.int32, (2 * slots, tokens), 0)
+    line = lax.broadcasted_iota(jnp.int32, (2 * slots, tokens), 0).astype(jnp.float32).astype(jnp.bfloat16)
+    one, zero = jnp.ones((), jnp.bfloat16), jnp.zeros((), jnp.bfloat16)
     for c in order + [0]:
         to = onto(c)
-        hot = jnp.where(line == slot - to * (2 * slots), 1.0, 0.0).astype(jnp.bfloat16)
+        mine = jnp.clip(slot - to * (2 * slots), -1, 2 * slots).astype(jnp.float32).astype(jnp.bfloat16)
+        hot = jnp.where(line == mine, one, zero)
         packed = lax.dot_general(token_rows, hot, NT, preferred_element_type=jnp.float32).astype(jnp.bfloat16)
         halves = [packed[:, :slots], packed[:, slots:]]
         if c == order[0]:
@@ -225,9 +228,12 @@
             squares = squares + tile * tile
             gath[ch, block_rows(blk), pl.ds(u * LANES, LANES)] = tile.astype(jnp.bfloat16)
         for c in order:
-            move(block(ch, blk), onto(c) * 2 + core, rg.at[ch, c])
+            move(block(ch, blk), onto(c) * 2 + core, rg.at[ch, c - 1])
         move(block(ch, blk), mate, rp.at[ch])
-    sq_out[...] = jnp.broadcast_to(jnp.sum(squares, axis=1, keepdims=True), (per, LANES))
+    diagonal = lax.broadcasted_iota(jnp.int32, (per, LANES), 0) == lax.broadcasted_iota(jnp.int32, (per, LANES), 1)
+    squares = jnp.broadcast_to(jnp.sum(squares, axis=1, keepdims=True), (per, LANES))
+    sq_out[...] = jnp.broadcast_to(
+        jnp.sum(jnp.where(diagonal, squares, 0.0), axis=0, keepdims=True), (SUBLANES, LANES))
 
     def square_copy(d):
         return pltpu.make_async_remote_copy(
@@ -236,7 +242,7 @@
 
     def total_copy(d, src):
         return pltpu.make_async_remote_copy(
-            src_ref=tot, dst_ref=norms.at[block_rows(src)], send_sem=st, recv_sem=rt,
+            src_ref=tot, dst_ref=norms.at[src], send_sem=st, recv_sem=rt,
             device_id={"blk": lax.rem(blk + d, blocks)}, device_id_type=pl.DeviceIdType.MESH)
 
     @pl.when(core == 1)
@@ -253,7 +259,7 @@
 
     def forward(ch, c):
         b = source(c) * 2 + core
-        wait_for(block(ch, b), rg.at[ch, c])
+        wait_for(block(ch, b), rg.at[ch, c - 1])
         move(block(ch, b), mate, rp.at[ch])
 
     def multiply(ch):
@@ -280,21 +286,23 @@
         for d in range(1, mods):
             total = total + sq_in[d]
         tot[...] = total
-        norms[block_rows(blk), :] = total
+        norms[blk] = total
         for d in range(1, blocks):
             total_copy(d, blk).start()
 
     for ch in range(CHUNKS):
         for at in range(ch + (ch > 0), min(ch + 2, CHUNKS)):
-            for c in order:
+            for c in order[1:] + order[:1]:
                 forward(at, c)
         if ch == 0:
             totals()
         if ch == CHUNKS - 1:
-            others = norms.at[pl.ds(0, docs - per)]
+            others = norms.at[pl.ds(0, blocks - 1)]
             wait_for(others, rt)
-            scale = 1.0 / jnp.sqrt(norms[...] + 1e-06)
-            inv[...] = jnp.concatenate([scale] * (WIDE // LANES), axis=1)
+            for b in range(blocks):
+                row = jnp.broadcast_to(norms[b, :1, :], (per, LANES))
+                total = jnp.sum(jnp.where(diagonal, row, 0.0), axis=1, keepdims=True)
+                inv[b * per:(b + 1) * per, :] = jnp.broadcast_to(1.0 / jnp.sqrt(total + 1e-06), (per, WIDE))
         multiply(ch)
     wait_for(send.at[pl.ds(0, blocks - 1)], sa)
     wait_for(gath.at[:, pl.ds(0, docs - per)], sg)
@@ -323,7 +331,7 @@
         in_specs=[hbm] * 7,
         out_specs=pl.BlockSpec(memory_space=pltpu.VMEM),
         scratch_shapes=[
-            pltpu.VMEM((docs, LANES), jnp.float32),
+            pltpu.VMEM((blocks, SUBLANES, LANES), jnp.float32),
             pltpu.VMEM((docs, WIDE), jnp.float32),
             pltpu.VMEM((square_of, 3 * square_of), jnp.bfloat16),
             pltpu.VMEM((1, tokens), jnp.int32),
@@ -338,12 +346,12 @@
             pltpu.VMEM((3 * WIDE, WIDE), jnp.bfloat16),
             pltpu.VMEM((per * g_dim * a_dim // LANES, LANES), jnp.float32),
             pltpu.VMEM((CHUNKS, docs, part), jnp.bfloat16),
-            pltpu.VMEM((per, LANES), jnp.float32),
-            pltpu.VMEM((mods, per, LANES), jnp.float32),
-            pltpu.VMEM((per, LANES), jnp.float32),
+            pltpu.VMEM((SUBLANES, LANES), jnp.float32),
+            pltpu.VMEM((mods, SUBLANES, LANES), jnp.float32),
+            pltpu.VMEM((SUBLANES, LANES), jnp.float32),
             dma(()), dma((6,)), pltpu.SemaphoreType.REGULAR,
             dma(()), dma((chips,)),
-            dma(()), dma((CHUNKS, chips)), dma((CHUNKS,)),
+            dma(()), dma((CHUNKS, chips - 1)), dma((CHUNKS,)),
             dma(()), dma(()), dma(()), dma(()),
         ],
         compiler_params=pltpu.CompilerParams(

time: 21.7 us -> 21.3 us (0.982)
  Pallas kernels: 20.1 us -> 19.8 us
    pallas_call x1, Pallas kernels: 20.1 us -> 19.8 us  [body(): pl.pallas_call(functools.partial(kernel, blocks, mods), out_shape=pltpu.V...]
where the time goes in v3:
time: 21.3 us; the launch traced here: 21.2 us
  Pallas kernels  19.8 us (93%)
  local copies, waits for them, and re-layouts  1.32 us (6%)
    pallas_call x1, Pallas kernels, body(): pl.pallas_call(functools.partial(kernel, blocks, mods), out_shape=pltpu.V...  19.8 us
    unnamed x1, local copies, waits for them, and re-layouts  1.32 us

profile of v3, /device:TPU:0, one launch (start us, length us, event | category | flops | bytes accessed | tf_op | source)
XLA Modules:
  0.0 21.2 jit_solution(18078444336769799073)
XLA Ops:
  0.0 19.8 %shard_map.73 = f32[256,2048]{1,0:T(8,128)S(1)} custom-call(s32[1,1024]{1,0:T(1,128)} %bitcast.14, s32[1,256]{1,0:T(1,128)} %bitcast.15, bf16[32,1024]{1,0:T(8,128)(2,1)} %bitcast.11, bf16[64,1024]{1,0:T(8,128)(2,1)} %bitcast.10, f32[64,64]{1,0:T(8,128)} %bitcast.12, f32[32,32]{1,0:T(8,128)} %bitcast.13, bf16[2048,2048]{1,0:T(8,128)(2,1)} %bitcast.9), custom_call_target="tpu_custom_call" | custom-call | tf_op jit(solution)/shard_map/pallas_call | solution.py:328
  19.8 1.3 %copy.9 = f32[1,256,2048]{2,1,0:T(8,128)} copy(f32[1,256,2048]{2,1,0:T(8,128)S(1)} %bitcast.8) | data formatting | bytes 4194304

commit v4 on v3

--- a/solution.py
+++ b/solution.py
@@ -9,13 +9,13 @@
 
 MOST = 4
 LANES = 128
+HALVES = 2
 SUBLANES = 8
 WIDE = 256
 CHUNKS = 4
 UNROLL = 8
 NT = (((1,), (1,)), ((), ()))
 TN = (((0,), (0,)), ((), ()))
-HIGH = lax.Precision.HIGHEST
 
 
 def kernel(
@@ -149,10 +149,15 @@
     low = (right - high.astype(jnp.float32)).astype(jnp.bfloat16)
     kin[...] = jnp.concatenate([high, high, low], axis=0)
     left = jnp.concatenate([pre_out_ref[pl.ds(i, steps, stride=packs), :] for i in range(packs)], axis=0)
-    wide_left = jnp.concatenate([left] * groups, axis=0)
+    short = steps // HALVES
+    bands = packs * short
+    wide_left = jnp.concatenate(
+        [left[i * steps + n * short:i * steps + (n + 1) * short]
+         for n in range(HALVES) for _ in range(groups) for i in range(packs)], axis=0)
     row_q = lax.broadcasted_iota(jnp.int32, (groups * g_dim, groups * g_dim), 0)
     col_q = lax.broadcasted_iota(jnp.int32, (groups * g_dim, groups * g_dim), 1)
-    wide_left = jnp.where(row_q // g_dim == col_q // g_dim, jnp.concatenate([wide_left] * groups, axis=1), 0.0)
+    wide_left = jnp.where(
+        (row_q % (groups * bands)) // bands == col_q // g_dim, jnp.concatenate([wide_left] * groups, axis=1), 0.0)
     high = wide_left.astype(jnp.bfloat16)
     low = (wide_left - high.astype(jnp.float32)).astype(jnp.bfloat16)
     kout[...] = jnp.concatenate([high, high, low], axis=1)
@@ -187,22 +192,27 @@
     half = jnp.dot(jnp.concatenate([high, low, high], axis=1), kin[...], preferred_element_type=jnp.float32)
     high = half.astype(jnp.bfloat16)
     low = (half - high.astype(jnp.float32)).astype(jnp.bfloat16)
-    cond = jnp.dot(kout[...], jnp.concatenate([high, low, high], axis=0), preferred_element_type=jnp.float32)
+    half = jnp.concatenate([high, low, high], axis=0)
 
     rows = groups * steps
-    lane_pack = lax.broadcasted_iota(jnp.int32, (rows, LANES), 1) // a_dim
-    for side in range(WIDE // LANES):
-        outs = [None] * packs
-        for i in range(packs):
-            x = jnp.concatenate(
-                [cond[q * g_dim + i * steps:q * g_dim + (i + 1) * steps, side * LANES:(side + 1) * LANES]
-                 for q in range(groups)], axis=0)
+    lane_pack = lax.broadcasted_iota(jnp.int32, (groups * short, LANES), 1) // a_dim
+
+    def lay_out(n):
+        cond = jnp.dot(kout[n * groups * bands:(n + 1) * groups * bands, :], half, preferred_element_type=jnp.float32)
+        for side in range(WIDE // LANES):
+            outs = [None] * packs
+            for i in range(packs):
+                x = jnp.concatenate(
+                    [cond[q * bands + i * short:q * bands + (i + 1) * short, side * LANES:(side + 1) * LANES]
+                     for q in range(groups)], axis=0)
+                for pos in range(packs):
+                    turn = ((i - pos) % packs) * a_dim
+                    moved = pltpu.roll(x, turn, 1) if turn else x
+                    outs[pos] = moved if outs[pos] is None else jnp.where(lane_pack == i, moved, outs[pos])
             for pos in range(packs):
-                turn = ((i - pos) % packs) * a_dim
-                moved = pltpu.roll(x, turn, 1) if turn else x
-                outs[pos] = moved if outs[pos] is None else jnp.where(lane_pack == i, moved, outs[pos])
-        for pos in range(packs):
-            lay[pl.ds((side * packs + pos) * rows, rows), :] = outs[pos]
+                for q in range(groups):
+                    lay[pl.ds((side * packs + pos) * rows + q * steps + n * short, short), :] = (
+                        outs[pos][q * short:(q + 1) * short])
 
     def block_rows(b):
         return pl.ds(pl.multiple_of(b * per, per), per)
@@ -221,6 +231,8 @@
     squares = jnp.zeros((per, LANES), jnp.float32)
     per_chunk = part // LANES
     for ch in range(CHUNKS):
+        if ch % (CHUNKS // HALVES) == 0:
+            lay_out(ch // (CHUNKS // HALVES))
         for u in range(per_chunk):
             j = ch * per_chunk + u
             tile = jnp.concatenate(

time: 21.3 us -> 21.2 us (level)
  no operation moved by 1% of the time
where the time goes in v4:
time: 21.2 us; the launch traced here: 21 us
  Pallas kernels  19.7 us (93%)
  local copies, waits for them, and re-layouts  1.32 us (6%)
    pallas_call x1, Pallas kernels, body(): pl.pallas_call(functools.partial(kernel, blocks, mods), out_shape=pltpu.V...  19.7 us
    unnamed x1, local copies, waits for them, and re-layouts  1.32 us

profile of v4, /device:TPU:0, one launch (start us, length us, event | category | flops | bytes accessed | tf_op | source)
XLA Modules:
  0.0 21.0 jit_solution(11032023287318092689)
XLA Ops:
  0.0 19.7 %shard_map.73 = f32[256,2048]{1,0:T(8,128)S(1)} custom-call(s32[1,1024]{1,0:T(1,128)} %bitcast.14, s32[1,256]{1,0:T(1,128)} %bitcast.15, bf16[32,1024]{1,0:T(8,128)(2,1)} %bitcast.11, bf16[64,1024]{1,0:T(8,128)(2,1)} %bitcast.10, f32[64,64]{1,0:T(8,128)} %bitcast.12, f32[32,32]{1,0:T(8,128)} %bitcast.13, bf16[2048,2048]{1,0:T(8,128)(2,1)} %bitcast.9), custom_call_target="tpu_custom_call" | custom-call | tf_op jit(solution)/shard_map/pallas_call | solution.py:340
  19.7 1.3 %copy.9 = f32[1,256,2048]{2,1,0:T(8,128)} copy(f32[1,256,2048]{2,1,0:T(8,128)S(1)} %bitcast.8) | data formatting | bytes 4194304
